TPU v7x, 256 devices: a whole 4x4x8 slice. The times are simulated.
256 devices in a mesh: swap: 16 (over y_hi, z), blk: 16 (over x, y_lo, core).
Axes of the slice: x: 4, y: 4 (y_hi: 2, y_lo: 2; y = y_hi * 2 + y_lo), z: 8, core: 2. Of those that a mesh axis runs over, the one named last changes fastest.
Arguments:
- queries: bfloat16 [32768, 4096], P(('blk', 'swap')), may hold values from -6 to 6
- keys: bfloat16 [32768, 512], P(('blk', 'swap')), may hold values from -6 to 6
- values: bfloat16 [32768, 512], P(('blk', 'swap')), may hold values from -6 to 6
- grad_out: bfloat16 [32768, 4096], P(('blk', 'swap')), may hold values from -6 to 6
- doc_ids: int32 [32768], replicated, may hold values from 0 to 32767, as said below
Outputs:
- grad_queries: bfloat16 [32768, 4096], P(('blk', 'swap'))
- grad_keys: bfloat16 [32768, 512], P(('blk', 'swap'))
- grad_values: bfloat16 [32768, 512], P(('blk', 'swap'))
Inputs may be any that keep to these rules, and one draw needn't show every extreme that they name: `doc_ids`: each token's label is the position of the first token of its document, so labels never fall along the sequence; each document holds 1 to 1024 tokens, the last token is a document of its own, and in every draw a document of exactly 1024 tokens ends on the first token of some block of 2048 tokens after the first block.
All inputs are finite; a program needn't handle non-finite values.
Results may differ from a plain program's by a relative error of at most 0.0058.
Values may be sent and summed in bfloat16 or wider, within the bound.
A program may use at most 64 MiB of HBM per device.

v0:
```python
import math

import jax
import jax.numpy as jnp
from jax import lax
from jax.sharding import PartitionSpec as P

HEAD_DIM = 128
MOST = 1024


masked_value = -1e30


def passed_along(block, axis, distance):
    devices = range(lax.axis_size(axis))
    route = [(i - distance, i) for i in devices if i - distance in devices]
    return lax.ppermute(block, axis, route)


def body(queries, keys, values, grad_out, doc_ids):
    inv_root = 1.0 / math.sqrt(HEAD_DIM)
    tok_rows = queries.shape[0]
    swap_size = lax.axis_size("swap")
    head_total = queries.shape[1] // HEAD_DIM
    kv_total = keys.shape[1] // HEAD_DIM
    heads_here = head_total // swap_size
    repeats = swap_size // kv_total
    seq_blk = tok_rows * swap_size
    k_slots = jnp.repeat(keys.reshape(tok_rows, kv_total, HEAD_DIM), repeats, axis=1).reshape(
        tok_rows, swap_size * HEAD_DIM
    )
    v_slots = jnp.repeat(values.reshape(tok_rows, kv_total, HEAD_DIM), repeats, axis=1).reshape(
        tok_rows, swap_size * HEAD_DIM
    )
    q_heads, g_heads, k_block, v_block = (
        lax.all_to_all(queries, "swap", split_axis=1, concat_axis=0, tiled=True),
        lax.all_to_all(grad_out, "swap", split_axis=1, concat_axis=0, tiled=True),
        lax.all_to_all(k_slots, "swap", split_axis=1, concat_axis=0, tiled=True),
        lax.all_to_all(v_slots, "swap", split_axis=1, concat_axis=0, tiled=True),
    )
    rim_k, rim_v = passed_along((k_block, v_block), "blk", 1)
    rim_len = rim_k.shape[0]
    k_all = jnp.concatenate([rim_k, k_block], 0)
    v_all = jnp.concatenate([rim_v, v_block], 0)
    block_start = lax.axis_index("blk") * seq_blk
    doc_padded = jnp.concatenate([jnp.full((MOST,), -1, jnp.int32), doc_ids], 0)
    tile_rows = min(512, seq_blk)
    key_width = MOST + tile_rows
    tile_count = seq_blk // tile_rows
    q_place = jnp.arange(tile_rows, dtype=jnp.int32)
    k_place = jnp.arange(key_width, dtype=jnp.int32) - MOST

    def tile_step(step_index, running):
        dq_acc, dk_acc, dv_acc = running
        tile_start = step_index * tile_rows
        key_start = rim_len + tile_start - MOST
        q_tile = lax.dynamic_slice_in_dim(q_heads, tile_start, tile_rows, 0).reshape(
            tile_rows, heads_here, HEAD_DIM
        )
        g_tile = lax.dynamic_slice_in_dim(g_heads, tile_start, tile_rows, 0).reshape(
            tile_rows, heads_here, HEAD_DIM
        )
        k_tile = lax.dynamic_slice_in_dim(k_all, key_start, key_width, 0)
        v_tile = lax.dynamic_slice_in_dim(v_all, key_start, key_width, 0)
        q_docs = lax.dynamic_slice_in_dim(doc_ids, block_start + tile_start, tile_rows, 0)
        k_docs = lax.dynamic_slice_in_dim(doc_padded, block_start + tile_start, key_width, 0)
        allowed = (k_place[None, :] <= q_place[:, None]) & (k_docs[None, :] == q_docs[:, None])
        scores = (
            jnp.einsum("qhd,kd->hqk", q_tile, k_tile, preferred_element_type=jnp.float32) * inv_root
        )
        scores = jnp.where(allowed, scores, masked_value)
        row_max = jnp.max(scores, axis=-1, keepdims=True)
        raised = jnp.exp(scores - row_max)
        weights = raised / jnp.sum(raised, axis=-1, keepdims=True)
        weights_b = weights.astype(jnp.bfloat16)
        attended = jnp.einsum("hqk,kd->qhd", weights_b, v_tile, preferred_element_type=jnp.float32)
        row_dot = jnp.sum(g_tile.astype(jnp.float32) * attended, axis=-1)
        dweights = jnp.einsum("qhd,kd->hqk", g_tile, v_tile, preferred_element_type=jnp.float32)
        d_scores = (weights * (dweights - jnp.transpose(row_dot)[:, :, None])).astype(jnp.bfloat16)
        dq_tile = (
            jnp.einsum("hqk,kd->qhd", d_scores, k_tile, preferred_element_type=jnp.float32)
            * inv_root
        )
        dq_tile = dq_tile.astype(jnp.bfloat16).reshape(tile_rows, heads_here * HEAD_DIM)
        dk_tile = (
            jnp.einsum("hqk,qhd->kd", d_scores, q_tile, preferred_element_type=jnp.float32)
            * inv_root
        )
        dv_tile = jnp.einsum("hqk,qhd->kd", weights_b, g_tile, preferred_element_type=jnp.float32)
        dq_acc = lax.dynamic_update_slice_in_dim(dq_acc, dq_tile, tile_start, 0)
        dk_acc = lax.dynamic_update_slice_in_dim(
            dk_acc,
            lax.dynamic_slice_in_dim(dk_acc, key_start, key_width, 0) + dk_tile,
            key_start,
            0,
        )
        dv_acc = lax.dynamic_update_slice_in_dim(
            dv_acc,
            lax.dynamic_slice_in_dim(dv_acc, key_start, key_width, 0) + dv_tile,
            key_start,
            0,
        )
        return (dq_acc, dk_acc, dv_acc)

    dq_start = jnp.zeros((seq_blk, heads_here * HEAD_DIM), jnp.bfloat16)
    kv_start = jnp.zeros((rim_len + seq_blk, HEAD_DIM), jnp.float32)
    dq_heads, dk_acc, dv_acc = lax.fori_loop(
        0, tile_count, tile_step, (dq_start, kv_start, kv_start)
    )
    back_k, back_v = passed_along((dk_acc[:rim_len], dv_acc[:rim_len]), "blk", -1)
    offset = seq_blk - rim_len
    own_k = dk_acc[rim_len:].at[offset:].add(back_k)
    own_v = dv_acc[rim_len:].at[offset:].add(back_v)
    grad_queries = lax.all_to_all(dq_heads, "swap", split_axis=0, concat_axis=1, tiled=True)
    k_home, v_home = (
        lax.all_to_all(own_k, "swap", split_axis=0, concat_axis=1, tiled=True),
        lax.all_to_all(own_v, "swap", split_axis=0, concat_axis=1, tiled=True),
    )
    grad_keys = (
        k_home.reshape(tok_rows, kv_total, repeats, HEAD_DIM)
        .sum(axis=2)
        .reshape(tok_rows, kv_total * HEAD_DIM)
        .astype(jnp.bfloat16)
    )
    grad_values = (
        v_home.reshape(tok_rows, kv_total, repeats, HEAD_DIM)
        .sum(axis=2)
        .reshape(tok_rows, kv_total * HEAD_DIM)
        .astype(jnp.bfloat16)
    )
    return (grad_queries, grad_keys, grad_values)


def solution(mesh):
    return jax.shard_map(
        body,
        mesh=mesh,
        in_specs=(
            P(("blk", "swap"), None),
            P(("blk", "swap"), None),
            P(("blk", "swap"), None),
            P(("blk", "swap"), None),
            P(),
        ),
        out_specs=(P(("blk", "swap"), None), P(("blk", "swap"), None), P(("blk", "swap"), None)),
        check_vma=False,
    )
```

profile of v0, /device:TPU:4, one launch (start us, length us, event | category | flops | bytes accessed | tf_op | source)
XLA Modules:
  0.0 319.9 jit_solution(1543017616225367761)
XLA Ops:
  2.5 11.2 %all-to-all-start.2 = ((bf16[128,16,128]{2,0,1:T(8,128)(2,1)}), bf16[128,16,128]{2,0,1:T(8,128)(2,1)S(1)}, u32[]{:S(2)}, u32[]{:S(2)}) async-start(bf16[128,16,128]{2,0,1:T(8,128)(2,1)} %bitcast.6), calls=%async_computation.2 | async-start | bytes 1048576 | tf_op jit(solution)/shard_map/all_to_all | solution.py:40
  14.7 16.2 %all-to-all-done.2 = bf16[128,16,128]{2,0,1:T(8,128)(2,1)S(1)} async-done(((bf16[128,16,128]{2,0,1:T(8,128)(2,1)}), bf16[128,16,128]{2,0,1:T(8,128)(2,1)S(1)}, u32[]{:S(2)}, u32[]{:S(2)}) %all-to-all-start.2) | async-done | bytes 524320 | tf_op jit(solution)/shard_map/all_to_all | solution.py:40
  31.8 4.5 %all-to-all-start = ((bf16[128,16,128]{2,0,1:T(8,128)(2,1)}), bf16[128,16,128]{2,0,1:T(8,128)(2,1)S(1)}, u32[]{:S(2)}, u32[]{:S(2)}) async-start(bf16[128,16,128]{2,0,1:T(8,128)(2,1)} %bitcast), calls=%async_computation | async-start | bytes 1048576 | tf_op jit(solution)/shard_map/all_to_all | solution.py:39
  37.6 14.7 %all-to-all-done = bf16[128,16,128]{2,0,1:T(8,128)(2,1)S(1)} async-done(((bf16[128,16,128]{2,0,1:T(8,128)(2,1)}), bf16[128,16,128]{2,0,1:T(8,128)(2,1)S(1)}, u32[]{:S(2)}, u32[]{:S(2)}) %all-to-all-start) | async-done | bytes 524320 | tf_op jit(solution)/shard_map/all_to_all | solution.py:39
  52.4 5.3 %all-to-all-start.1 = ((bf16[128,16,256]{0,2,1:T(8,128)(2,1)}), bf16[128,16,256]{0,2,1:T(8,128)(2,1)S(1)}, u32[]{:S(2)}, u32[]{:S(2)}) async-start(bf16[128,16,256]{0,2,1:T(8,128)(2,1)} %bitcast.3), calls=%async_computation.1 | async-start | bytes 2097152 | tf_op jit(solution)/shard_map/all_to_all | solution.py:37
  59.0 25.5 %all-to-all-done.1 = bf16[128,16,256]{0,2,1:T(8,128)(2,1)S(1)} async-done(((bf16[128,16,256]{0,2,1:T(8,128)(2,1)}), bf16[128,16,256]{0,2,1:T(8,128)(2,1)S(1)}, u32[]{:S(2)}, u32[]{:S(2)}) %all-to-all-start.1) | async-done | bytes 1048608 | tf_op jit(solution)/shard_map/all_to_all | solution.py:37
  84.5 4.9 %all-to-all-start.3 = ((bf16[128,16,256]{0,2,1:T(8,128)(2,1)}), bf16[128,16,256]{0,2,1:T(8,128)(2,1)S(1)}, u32[]{:S(2)}, u32[]{:S(2)}) async-start(bf16[128,16,256]{0,2,1:T(8,128)(2,1)} %bitcast.9), calls=%async_computation.3 | async-start | bytes 2097152 | tf_op jit(solution)/shard_map/all_to_all | solution.py:38
  89.4 1.9 collective-permute-start
  91.4 2.7 collective-permute-start.1
  94.1 11.0 %collective-permute-done = bf16[2048,128]{1,0:T(8,128)(2,1)} collective-permute-done((bf16[2048,128]{1,0:T(8,128)(2,1)S(1)}, bf16[2048,128]{1,0:T(8,128)(2,1)}, u32[]{:S(2)}, u32[]{:S(2)}) %collective-permute-start) | collective-permute-done | bytes 524320 | tf_op jit(solution)/shard_map/ppermute | solution.py:18
  105.0 2.2 pad_maximum_fusion
  107.2 7.4 %collective-permute-done.1 = bf16[2048,128]{1,0:T(8,128)(2,1)} collective-permute-done((bf16[2048,128]{1,0:T(8,128)(2,1)S(1)}, bf16[2048,128]{1,0:T(8,128)(2,1)}, u32[]{:S(2)}, u32[]{:S(2)}) %collective-permute-start.1) | collective-permute-done | bytes 524320 | tf_op jit(solution)/shard_map/ppermute | solution.py:18
  114.7 2.1 pad_maximum_fusion.1
  118.1 1.3 copy.57
  120.6 1.5 broadcast_in_dim.63
  122.1 87.1 %while.26 = (s32[]{:T(128)}, bf16[2048,256]{1,0:T(8,128)(2,1)}, f32[4096,128]{1,0:T(8,128)}, f32[4096,128]{1,0:T(8,128)S(1)}, bf16[4096,128]{1,0:T(8,128)(2,1)},...) while((s32[]{:T(128)}, bf16[2048,256]{1,0:T(8,128)(2,1)}, ...), condition=%wide.region_4.5_spmd.clone, body=%wide.region_0.4_spmd.clone.sunk | while | flops 2435254272 | bytes 90268256 | solution.py:108
  124.2 2.0 fusion.91
  126.1 6.1 %fusion.92 = (f32[2,512]{1,0:T(2,128)S(1)}, f32[2,512,1536]{1,2,0:T(8,128)}) fusion(pred[512,1536]{0,1:T(8,128)(4,1)S(1)} %fusion.91, bf16[512,2,128]{0,2,1:T(8,128)(2,1)S(1)} %bitcast.156, bf16[4096,128]{1,0:T(8,128)(2,1)} %get-tuple-element.632, s32[]{:T(128)S(6)} %select_n.93), kind=kOutput, calls=%fused_computation.59.clone.1 | convolution fusion | flops 408946176 | bytes 7737348 | tf_op jit(solution)/shard_map/while/body/eval_jaxpr/sub | solution.py:74
  132.3 3.9 %fusion.93 = bf16[2,512,1536]{1,2,0:T(8,128)(2,1)S(1)} fusion(f32[2,512,1536]{1,2,0:T(8,128)} %get-tuple-element.588, f32[2,512]{1,0:T(2,128)S(1)} %get-tuple-element.589), kind=kLoop, calls=%fused_computation.15.clone.1 | loop fusion | flops 3145728 | bytes 9441280 | tf_op jit(solution)/shard_map/while/body/eval_jaxpr/convert_element_type | solution.py:76
  138.8 1.8 fusion.96
  141.6 1.3 copy-done.2
  146.0 2.0 fusion.91
  147.9 6.1 %fusion.92 = (f32[2,512]{1,0:T(2,128)S(1)}, f32[2,512,1536]{1,2,0:T(8,128)}) fusion(pred[512,1536]{0,1:T(8,128)(4,1)S(1)} %fusion.91, bf16[512,2,128]{0,2,1:T(8,128)(2,1)S(1)} %bitcast.156, bf16[4096,128]{1,0:T(8,128)(2,1)} %get-tuple-element.632, s32[]{:T(128)S(6)} %select_n.93), kind=kOutput, calls=%fused_computation.59.clone.1 | convolution fusion | flops 408946176 | bytes 7737348 | tf_op jit(solution)/shard_map/while/body/eval_jaxpr/sub | solution.py:74
  154.1 3.9 %fusion.93 = bf16[2,512,1536]{1,2,0:T(8,128)(2,1)S(1)} fusion(f32[2,512,1536]{1,2,0:T(8,128)} %get-tuple-element.588, f32[2,512]{1,0:T(2,128)S(1)} %get-tuple-element.589), kind=kLoop, calls=%fused_computation.15.clone.1 | loop fusion | flops 3145728 | bytes 9441280 | tf_op jit(solution)/shard_map/while/body/eval_jaxpr/convert_element_type | solution.py:76
  160.6 1.8 fusion.96
  163.4 1.3 copy-done.2
  167.7 2.0 fusion.91
  169.7 6.1 %fusion.92 = (f32[2,512]{1,0:T(2,128)S(1)}, f32[2,512,1536]{1,2,0:T(8,128)}) fusion(pred[512,1536]{0,1:T(8,128)(4,1)S(1)} %fusion.91, bf16[512,2,128]{0,2,1:T(8,128)(2,1)S(1)} %bitcast.156, bf16[4096,128]{1,0:T(8,128)(2,1)} %get-tuple-element.632, s32[]{:T(128)S(6)} %select_n.93), kind=kOutput, calls=%fused_computation.59.clone.1 | convolution fusion | flops 408946176 | bytes 7737348 | tf_op jit(solution)/shard_map/while/body/eval_jaxpr/sub | solution.py:74
  175.8 3.9 %fusion.93 = bf16[2,512,1536]{1,2,0:T(8,128)(2,1)S(1)} fusion(f32[2,512,1536]{1,2,0:T(8,128)} %get-tuple-element.588, f32[2,512]{1,0:T(2,128)S(1)} %get-tuple-element.589), kind=kLoop, calls=%fused_computation.15.clone.1 | loop fusion | flops 3145728 | bytes 9441280 | tf_op jit(solution)/shard_map/while/body/eval_jaxpr/convert_element_type | solution.py:76
  182.4 1.8 fusion.96
  185.2 1.3 copy-done.2
  189.5 2.0 fusion.91
  191.5 6.1 %fusion.92 = (f32[2,512]{1,0:T(2,128)S(1)}, f32[2,512,1536]{1,2,0:T(8,128)}) fusion(pred[512,1536]{0,1:T(8,128)(4,1)S(1)} %fusion.91, bf16[512,2,128]{0,2,1:T(8,128)(2,1)S(1)} %bitcast.156, bf16[4096,128]{1,0:T(8,128)(2,1)} %get-tuple-element.632, s32[]{:T(128)S(6)} %select_n.93), kind=kOutput, calls=%fused_computation.59.clone.1 | convolution fusion | flops 408946176 | bytes 7737348 | tf_op jit(solution)/shard_map/while/body/eval_jaxpr/sub | solution.py:74
  197.6 3.9 %fusion.93 = bf16[2,512,1536]{1,2,0:T(8,128)(2,1)S(1)} fusion(f32[2,512,1536]{1,2,0:T(8,128)} %get-tuple-element.588, f32[2,512]{1,0:T(2,128)S(1)} %get-tuple-element.589), kind=kLoop, calls=%fused_computation.15.clone.1 | loop fusion | flops 3145728 | bytes 9441280 | tf_op jit(solution)/shard_map/while/body/eval_jaxpr/convert_element_type | solution.py:76
  204.2 1.8 fusion.96
  207.0 1.3 copy-done.2
  209.2 9.5 %all-to-all-start.4 = ((bf16[16,128,256]{2,1,0:T(8,128)(2,1)}), bf16[16,128,256]{2,1,0:T(8,128)(2,1)S(1)}, u32[]{:S(2)}, u32[]{:S(2)}) async-start(bf16[16,128,256]{2,1,0:T(8,128)(2,1)} %bitcast.160), calls=%async_computation.4 | async-start | bytes 2097152 | tf_op jit(solution)/shard_map/all_to_all | solution.py:115
  220.0 1.9 collective-permute-start.2
  221.9 19.3 %collective-permute-done.2 = f32[2048,128]{1,0:T(8,128)S(1)} collective-permute-done((f32[2048,128]{1,0:T(8,128)S(1)}, f32[2048,128]{1,0:T(8,128)S(1)}, u32[]{:S(2)}, u32[]{:S(2)}) %collective-permute-start.2) | collective-permute-done | bytes 1048608 | tf_op jit(solution)/shard_map/ppermute | solution.py:18
  241.2 2.3 slice_add_fusion.1
  243.5 1.9 all-to-all-done.4
  245.4 7.8 %all-to-all-start.5 = ((f32[16,128,128]{2,1,0:T(8,128)}), f32[16,128,128]{2,1,0:T(8,128)}, u32[]{:S(2)}, u32[]{:S(2)}) async-start(f32[16,128,128]{2,1,0:T(8,128)} %bitcast.15), calls=%async_computation.5 | async-start | bytes 2097152 | tf_op jit(solution)/shard_map/all_to_all | solution.py:117
  253.3 3.9 %collective-permute-start.3 = (f32[2048,128]{1,0:T(8,128)S(1)}, f32[2048,128]{1,0:T(8,128)S(1)}, u32[]{:S(2)}, u32[]{:S(2)}) collective-permute-start(f32[2048,128]{1,0:T(8,128)S(1)} %slice.43), channel_id=1, source_target_pairs={{1,0},{2,1},{3,2},{4,3},{5,4},{6,5},{7,6},{8,7},{9,8},{10,9},{11,1... | collective-permute-start | bytes 3145736 | tf_op jit(solution)/shard_map/ppermute | solution.py:18
  257.2 19.9 %collective-permute-done.3 = f32[2048,128]{1,0:T(8,128)S(1)} collective-permute-done((f32[2048,128]{1,0:T(8,128)S(1)}, f32[2048,128]{1,0:T(8,128)S(1)}, u32[]{:S(2)}, u32[]{:S(2)}) %collective-permute-start.3) | collective-permute-done | bytes 1048608 | tf_op jit(solution)/shard_map/ppermute | solution.py:18
  278.2 6.3 %all-to-all-done.5 = f32[16,128,128]{2,1,0:T(8,128)} async-done(((f32[16,128,128]{2,1,0:T(8,128)}), f32[16,128,128]{2,1,0:T(8,128)}, u32[]{:S(2)}, u32[]{:S(2)}) %all-to-all-start.5) | async-done | bytes 1048608 | tf_op jit(solution)/shard_map/all_to_all | solution.py:117
  284.5 5.5 %all-to-all-start.6 = ((f32[16,128,128]{2,1,0:T(8,128)}), f32[16,128,128]{2,1,0:T(8,128)S(1)}, u32[]{:S(2)}, u32[]{:S(2)}) async-start(f32[16,128,128]{2,1,0:T(8,128)} %bitcast.19), calls=%async_computation.6 | async-start | bytes 2097152 | tf_op jit(solution)/shard_map/all_to_all | solution.py:118
  290.6 1.3 copy.64
  294.1 24.8 %all-to-all-done.6 = f32[16,128,128]{2,1,0:T(8,128)S(1)} async-done(((f32[16,128,128]{2,1,0:T(8,128)}), f32[16,128,128]{2,1,0:T(8,128)S(1)}, u32[]{:S(2)}, u32[]{:S(2)}) %all-to-all-start.6) | async-done | bytes 1048608 | tf_op jit(solution)/shard_map/all_to_all | solution.py:118
  (141 shorter events, 41.5 us)
Async XLA Ops:
  0.6 0.9 copy-start
  0.6 35.7 %copy-start.4 = (bf16[128,4096]{1,0:T(8,128)(2,1)S(1)}, bf16[128,4096]{1,0:T(8,128)(2,1)}, u32[]{:S(2)}) copy-start(bf16[128,4096]{1,0:T(8,128)(2,1)} %param.15) | copy-start | bytes 3145732
  2.5 28.4 %all-to-all-start.2 = ((bf16[128,16,128]{2,0,1:T(8,128)(2,1)}), bf16[128,16,128]{2,0,1:T(8,128)(2,1)S(1)}, u32[]{:S(2)}, u32[]{:S(2)}) async-start(bf16[128,16,128]{2,0,1:T(8,128)(2,1)} %bitcast.6), calls=%async_computation.2 | async-start | bytes 1048576 | tf_op jit(solution)/shard_map/all_to_all | solution.py:40
  13.7 44.0 %copy-start.5 = (bf16[128,4096]{1,0:T(8,128)(2,1)S(1)}, bf16[128,4096]{1,0:T(8,128)(2,1)}, u32[]{:S(2)}) copy-start(bf16[128,4096]{1,0:T(8,128)(2,1)} %param.18) | copy-start | bytes 3145732
  31.8 20.6 %all-to-all-start = ((bf16[128,16,128]{2,0,1:T(8,128)(2,1)}), bf16[128,16,128]{2,0,1:T(8,128)(2,1)S(1)}, u32[]{:S(2)}, u32[]{:S(2)}) async-start(bf16[128,16,128]{2,0,1:T(8,128)(2,1)} %bitcast), calls=%async_computation | async-start | bytes 1048576 | tf_op jit(solution)/shard_map/all_to_all | solution.py:39
  52.4 41.7 %copy-start.8 = (s32[32768]{0:T(1024)S(1)}, s32[32768]{0:T(1024)}, u32[]{:S(2)}) copy-start(s32[32768]{0:T(1024)} %param.19) | copy-start | bytes 393220
  52.4 32.1 %all-to-all-start.1 = ((bf16[128,16,256]{0,2,1:T(8,128)(2,1)}), bf16[128,16,256]{0,2,1:T(8,128)(2,1)S(1)}, u32[]{:S(2)}, u32[]{:S(2)}) async-start(bf16[128,16,256]{0,2,1:T(8,128)(2,1)} %bitcast.3), calls=%async_computation.1 | async-start | bytes 2097152 | tf_op jit(solution)/shard_map/all_to_all | solution.py:37
  84.5 33.6 %all-to-all-start.3 = ((bf16[128,16,256]{0,2,1:T(8,128)(2,1)}), bf16[128,16,256]{0,2,1:T(8,128)(2,1)S(1)}, u32[]{:S(2)}, u32[]{:S(2)}) async-start(bf16[128,16,256]{0,2,1:T(8,128)(2,1)} %bitcast.9), calls=%async_computation.3 | async-start | bytes 2097152 | tf_op jit(solution)/shard_map/all_to_all | solution.py:38
  89.4 15.6 %collective-permute-start = (bf16[2048,128]{1,0:T(8,128)(2,1)S(1)}, bf16[2048,128]{1,0:T(8,128)(2,1)}, u32[]{:S(2)}, u32[]{:S(2)}) collective-permute-start(bf16[2048,128]{1,0:T(8,128)(2,1)S(1)} %bitcast.164), channel_id=1, source_target_pairs={{0,1},{1,2},{2,3},{3,4},{4,5},{5,6},{6,7},{7,8},{8,9},{9,10},{10,1... | collective-permute-start | bytes 1572872 | tf_op jit(solution)/shard_map/ppermute | solution.py:18
  91.4 23.3 %collective-permute-start.1 = (bf16[2048,128]{1,0:T(8,128)(2,1)S(1)}, bf16[2048,128]{1,0:T(8,128)(2,1)}, u32[]{:S(2)}, u32[]{:S(2)}) collective-permute-start(bf16[2048,128]{1,0:T(8,128)(2,1)S(1)} %bitcast.162), channel_id=1, source_target_pairs={{0,1},{1,2},{2,3},{3,4},{4,5},{5,6},{6,7},{7,8},{8,9},{9,10},{10,1... | collective-permute-start | bytes 1572872 | tf_op jit(solution)/shard_map/ppermute | solution.py:18
  122.1 2.1 copy-start.6
  132.3 3.9 %copy-start.3 = (bf16[4096,128]{1,0:T(8,128)(2,1)S(1)}, bf16[4096,128]{1,0:T(8,128)(2,1)}, u32[]{:S(2)}) copy-start(bf16[4096,128]{1,0:T(8,128)(2,1)} %get-tuple-element.637) | copy-start | bytes 3145732 | tf_op jit(solution)/shard_map/while
  132.3 5.5 %slice-start = ((s8[6291456]{0:T(1024)(128)(4,1)}), s8[4194304]{0:T(1024)(128)(4,1)S(1)}, s32[]{:S(2)}) async-start(s8[6291456]{0:T(1024)(128)(4,1)} %bitcast.150), calls=%async_computation.7 | async-start | bytes 8388608 | tf_op jit(solution)/shard_map/while
  136.2 1.7 slice-start.1
  138.8 1.8 copy-start.1
  140.6 3.2 %copy-start.7 = (s32[33792]{0:T(1024)S(1)}, s32[33792]{0:T(1024)}, u32[]{:S(2)}) copy-start(s32[33792]{0:T(1024)} %copy-done.6) | copy-start | bytes 405508 | tf_op jit(solution)/shard_map/while
  140.6 3.2 %copy-start.9 = (s32[32768]{0:T(1024)S(1)}, s32[32768]{0:T(1024)}, u32[]{:S(2)}) copy-start(s32[32768]{0:T(1024)} %get-tuple-element.680) | copy-start | bytes 393220 | tf_op jit(solution)/shard_map/while
  141.6 1.4 copy-start.2
  143.9 2.1 copy-start.6
  154.1 3.9 %copy-start.3 = (bf16[4096,128]{1,0:T(8,128)(2,1)S(1)}, bf16[4096,128]{1,0:T(8,128)(2,1)}, u32[]{:S(2)}) copy-start(bf16[4096,128]{1,0:T(8,128)(2,1)} %get-tuple-element.637) | copy-start | bytes 3145732 | tf_op jit(solution)/shard_map/while
  154.1 5.5 %slice-start = ((s8[6291456]{0:T(1024)(128)(4,1)}), s8[4194304]{0:T(1024)(128)(4,1)S(1)}, s32[]{:S(2)}) async-start(s8[6291456]{0:T(1024)(128)(4,1)} %bitcast.150), calls=%async_computation.7 | async-start | bytes 8388608 | tf_op jit(solution)/shard_map/while
  157.9 1.7 slice-start.1
  160.6 1.8 copy-start.1
  162.4 3.2 %copy-start.7 = (s32[33792]{0:T(1024)S(1)}, s32[33792]{0:T(1024)}, u32[]{:S(2)}) copy-start(s32[33792]{0:T(1024)} %copy-done.6) | copy-start | bytes 405508 | tf_op jit(solution)/shard_map/while
  162.4 3.2 %copy-start.9 = (s32[32768]{0:T(1024)S(1)}, s32[32768]{0:T(1024)}, u32[]{:S(2)}) copy-start(s32[32768]{0:T(1024)} %get-tuple-element.680) | copy-start | bytes 393220 | tf_op jit(solution)/shard_map/while
  163.4 1.4 copy-start.2
  165.6 2.1 copy-start.6
  175.8 3.9 %copy-start.3 = (bf16[4096,128]{1,0:T(8,128)(2,1)S(1)}, bf16[4096,128]{1,0:T(8,128)(2,1)}, u32[]{:S(2)}) copy-start(bf16[4096,128]{1,0:T(8,128)(2,1)} %get-tuple-element.637) | copy-start | bytes 3145732 | tf_op jit(solution)/shard_map/while
  175.8 5.5 %slice-start = ((s8[6291456]{0:T(1024)(128)(4,1)}), s8[4194304]{0:T(1024)(128)(4,1)S(1)}, s32[]{:S(2)}) async-start(s8[6291456]{0:T(1024)(128)(4,1)} %bitcast.150), calls=%async_computation.7 | async-start | bytes 8388608 | tf_op jit(solution)/shard_map/while
  179.7 1.7 slice-start.1
  182.4 1.8 copy-start.1
  184.2 3.2 %copy-start.7 = (s32[33792]{0:T(1024)S(1)}, s32[33792]{0:T(1024)}, u32[]{:S(2)}) copy-start(s32[33792]{0:T(1024)} %copy-done.6) | copy-start | bytes 405508 | tf_op jit(solution)/shard_map/while
  184.2 3.2 %copy-start.9 = (s32[32768]{0:T(1024)S(1)}, s32[32768]{0:T(1024)}, u32[]{:S(2)}) copy-start(s32[32768]{0:T(1024)} %get-tuple-element.680) | copy-start | bytes 393220 | tf_op jit(solution)/shard_map/while
  185.2 1.4 copy-start.2
  187.4 2.1 copy-start.6
  197.6 3.9 %copy-start.3 = (bf16[4096,128]{1,0:T(8,128)(2,1)S(1)}, bf16[4096,128]{1,0:T(8,128)(2,1)}, u32[]{:S(2)}) copy-start(bf16[4096,128]{1,0:T(8,128)(2,1)} %get-tuple-element.637) | copy-start | bytes 3145732 | tf_op jit(solution)/shard_map/while
  197.6 5.5 %slice-start = ((s8[6291456]{0:T(1024)(128)(4,1)}), s8[4194304]{0:T(1024)(128)(4,1)S(1)}, s32[]{:S(2)}) async-start(s8[6291456]{0:T(1024)(128)(4,1)} %bitcast.150), calls=%async_computation.7 | async-start | bytes 8388608 | tf_op jit(solution)/shard_map/while
  201.5 1.7 slice-start.1
  204.2 1.8 copy-start.1
  206.0 3.2 %copy-start.7 = (s32[33792]{0:T(1024)S(1)}, s32[33792]{0:T(1024)}, u32[]{:S(2)}) copy-start(s32[33792]{0:T(1024)} %copy-done.6) | copy-start | bytes 405508 | tf_op jit(solution)/shard_map/while
  206.0 3.2 %copy-start.9 = (s32[32768]{0:T(1024)S(1)}, s32[32768]{0:T(1024)}, u32[]{:S(2)}) copy-start(s32[32768]{0:T(1024)} %get-tuple-element.680) | copy-start | bytes 393220 | tf_op jit(solution)/shard_map/while
  207.0 1.4 copy-start.2
  209.2 36.2 %all-to-all-start.4 = ((bf16[16,128,256]{2,1,0:T(8,128)(2,1)}), bf16[16,128,256]{2,1,0:T(8,128)(2,1)S(1)}, u32[]{:S(2)}, u32[]{:S(2)}) async-start(bf16[16,128,256]{2,1,0:T(8,128)(2,1)} %bitcast.160), calls=%async_computation.4 | async-start | bytes 2097152 | tf_op jit(solution)/shard_map/all_to_all | solution.py:115
  220.0 21.2 %collective-permute-start.2 = (f32[2048,128]{1,0:T(8,128)S(1)}, f32[2048,128]{1,0:T(8,128)S(1)}, u32[]{:S(2)}, u32[]{:S(2)}) collective-permute-start(f32[2048,128]{1,0:T(8,128)S(1)} %slice.41), channel_id=1, source_target_pairs={{1,0},{2,1},{3,2},{4,3},{5,4},{6,5},{7,6},{8,7},{9,8},{10,9},{11,1... | collective-permute-start | bytes 3145736 | tf_op jit(solution)/shard_map/ppermute | solution.py:18
  245.4 39.1 %all-to-all-start.5 = ((f32[16,128,128]{2,1,0:T(8,128)}), f32[16,128,128]{2,1,0:T(8,128)}, u32[]{:S(2)}, u32[]{:S(2)}) async-start(f32[16,128,128]{2,1,0:T(8,128)} %bitcast.15), calls=%async_computation.5 | async-start | bytes 2097152 | tf_op jit(solution)/shard_map/all_to_all | solution.py:117
  253.3 23.8 %collective-permute-start.3 = (f32[2048,128]{1,0:T(8,128)S(1)}, f32[2048,128]{1,0:T(8,128)S(1)}, u32[]{:S(2)}, u32[]{:S(2)}) collective-permute-start(f32[2048,128]{1,0:T(8,128)S(1)} %slice.43), channel_id=1, source_target_pairs={{1,0},{2,1},{3,2},{4,3},{5,4},{6,5},{7,6},{8,7},{9,8},{10,9},{11,1... | collective-permute-start | bytes 3145736 | tf_op jit(solution)/shard_map/ppermute | solution.py:18
  284.5 34.5 %all-to-all-start.6 = ((f32[16,128,128]{2,1,0:T(8,128)}), f32[16,128,128]{2,1,0:T(8,128)S(1)}, u32[]{:S(2)}, u32[]{:S(2)}) async-start(f32[16,128,128]{2,1,0:T(8,128)} %bitcast.19), calls=%async_computation.6 | async-start | bytes 2097152 | tf_op jit(solution)/shard_map/all_to_all | solution.py:118
where the time goes:
time: 321 us; the launch traced here: 320 us
  waiting for transfers between devices  147 us (46%)
  starting transfers between devices  59.1 us (18%)
  matrix products  45.9 us (14%)
  local copies, waits for them, and re-layouts  34.2 us (11%)
  other arithmetic  32.3 us (10%)
    ppermute x4, waiting for transfers between devices, passed_along(): return lax.ppermute(block, axis, route)  57.6 us
    all_to_all x1, waiting for transfers between devices, body(): lax.all_to_all(queries, 'swap', split_axis=1, concat_axis=0, tiled=True)  25.5 us
    all_to_all x1, waiting for transfers between devices, body(): lax.all_to_all(own_v, 'swap', split_axis=0, concat_axis=1, tiled=True)  24.8 us
    sub x4, matrix products, tile_step(): raised = jnp.exp(scores - row_max)  24.5 us
    all_to_all x1, waiting for transfers between devices, body(): lax.all_to_all(v_slots, 'swap', split_axis=1, concat_axis=0, tiled=True)  16.2 us
    convert_element_type x4, other arithmetic, tile_step(): weights_b = weights.astype(jnp.bfloat16)  15.4 us
    all_to_all x1, waiting for transfers between devices, body(): lax.all_to_all(k_slots, 'swap', split_axis=1, concat_axis=0, tiled=True)  14.7 us
    all_to_all x1, starting transfers between devices, body(): lax.all_to_all(v_slots, 'swap', split_axis=1, concat_axis=0, tiled=True)  11.2 us
  transfers between devices with their start and end apart: 11, of which 10 were waited for; matrix products, arithmetic and copies ran while one was open for 6% of the time, Pallas kernels for 0%

commit v1 on v0

v1 whole, which is shorter than its diff:
```python
import functools
import math

import jax
import jax.numpy as jnp
from jax import lax
from jax.experimental import pallas as pl
from jax.experimental.pallas import tpu as pltpu
from jax.sharding import PartitionSpec as P

DIM = 128
REACH = 8
SLOTS = REACH + 1
MESH = pl.DeviceIdType.MESH
MASKED = -1e30
F32 = jnp.float32
BF16 = jnp.bfloat16


def contract(a, b, dims):
    return lax.dot_general(a, b, (dims, ((), ())), preferred_element_type=F32)


def kernel(
    blks, swaps, kv_heads, share,
    q_hbm, g_hbm, k_hbm, v_hbm, docs,
    dq_out, dk_out, dv_out,
    qv, gv, kvb, kt, bias, pf, dpf, pt, dst, acc, outbox, inbox,
    load_sem, own_sem, get_send, get_recv, put_send, put_recv,
):
    total = blks * swaps
    me = lax.axis_index("blk") * swaps + lax.axis_index("swap")
    inv_root = 1.0 / math.sqrt(DIM)
    to_exp2 = inv_root * math.log2(math.e)
    tiles = share // 2

    def device(offset):
        other = lax.rem(me + (offset + total), total)
        return {"blk": lax.div(other, swaps), "swap": lax.rem(other, swaps)}

    def own_copy(group, part):
        source = (k_hbm, v_hbm)[part]
        return pltpu.make_async_copy(
            source.at[:, pl.ds(group * DIM, DIM)],
            kvb.at[group, 0, :, pl.ds(part * DIM, DIM)],
            own_sem.at[group, part],
        )

    def get_copy(group, source, target, offset, lane):
        return pltpu.make_async_remote_copy(
            src_ref=kvb.at[group, source],
            dst_ref=kvb.at[group, target],
            send_sem=get_send.at[group, lane],
            recv_sem=get_recv.at[group, target],
            device_id=device(offset),
            device_id_type=MESH,
        )

    def put_copy(group, source, target, offset):
        return pltpu.make_async_remote_copy(
            src_ref=outbox.at[group, source],
            dst_ref=inbox.at[group, target],
            send_sem=put_send.at[group, source],
            recv_sem=put_recv.at[group, target],
            device_id=device(offset),
            device_id_type=MESH,
        )

    def get_wait(group, slot):
        get_copy(group, slot, slot, 1, 0).wait_recv()

    def put_wait(group, slot):
        put_copy(group, 1, slot, 1).wait_recv()

    def relay(group, level):
        near, far = level, SLOTS - level
        get_wait(group, near)
        get_copy(group, near, near + 1, 1, near).start()
        get_wait(group, far)
        get_copy(group, far, far - 1, -1, far - 1).start()

    def ship(group, near, far, first):
        for slot in (near, far):
            value = acc[group, slot]
            if not first:
                put_wait(group, slot)
                value = value + inbox[group, slot].astype(F32)
            outbox[group, slot] = value.astype(BF16)
            if slot == near:
                put_copy(group, slot, slot - 1, -1).start()
            elif slot < REACH:
                put_copy(group, slot, slot + 1, 1).start()
            else:
                put_copy(group, slot, slot + 1, -REACH).start()

    def settle(group):
        put_wait(group, 0)
        put_wait(group, SLOTS)
        value = acc[group, 0] + inbox[group, 0].astype(F32) + inbox[group, SLOTS].astype(F32)
        at = pl.multiple_of(group * DIM, DIM)
        dk_out[:, pl.ds(at, DIM)] = value[:, :DIM].astype(BF16)
        dv_out[:, pl.ds(at, DIM)] = value[:, DIM:].astype(BF16)

    q_load = pltpu.make_async_copy(q_hbm, qv, load_sem.at[0])
    g_load = pltpu.make_async_copy(g_hbm, gv, load_sem.at[1])
    for group in range(kv_heads):
        for part in range(2):
            own_copy(group, part).start()
    q_load.start()
    g_load.start()

    barrier = pltpu.get_barrier_semaphore()
    for offset in (1, -1, REACH, -REACH):
        pl.semaphore_signal(barrier, inc=1, device_id=device(offset), device_id_type=MESH)
    pl.semaphore_wait(barrier, 4)

    for group in range(kv_heads):
        for part in range(2):
            own_copy(group, part).wait()
        get_copy(group, 0, 1, 1, 0).start()
        get_copy(group, 0, REACH, REACH, REACH).start()

    q_docs = docs[pl.ds(me, 1), :].astype(F32)
    causal = lax.broadcasted_iota(jnp.int32, (DIM, DIM), 0) <= lax.broadcasted_iota(
        jnp.int32, (DIM, DIM), 1
    )
    for slot in range(SLOTS):
        row = docs[pl.ds(lax.rem(me + (total - slot), total), 1), :].astype(F32)
        row = jnp.where(me >= slot, row, -1.0)
        k_docs = jnp.transpose(jnp.broadcast_to(row, (DIM, DIM)))
        allowed = k_docs == q_docs
        if slot == 0:
            allowed = allowed & causal
        bias[slot] = jnp.where(allowed, 0.0, MASKED)
    q_load.wait()
    g_load.wait()

    for level in range(1, 4):
        relay(0, level)
        if level > 1 and kv_heads > 1:
            relay(1, level - 1)

    def stacked(ref, group, first, count):
        at = (group * share + first) * DIM
        return jnp.concatenate(
            [ref[:, pl.ds(pl.multiple_of(at + i * DIM, DIM), DIM)] for i in range(count)], 0
        )

    def tile(group, index):
        q_rows = stacked(qv, group, 2 * index, 2)
        g_rows = stacked(gv, group, 2 * index, 2)
        tops, sums, dots = [], [], []
        for slot in range(SLOTS):
            part = bias[slot]
            scores = contract(kvb[group, slot, :, :DIM], q_rows, ((1,), (1,)))
            dweights = contract(kvb[group, slot, :, DIM:], g_rows, ((1,), (1,)))
            scores = scores * to_exp2 + jnp.concatenate([part, part], 1)
            top = jnp.max(scores, 0, keepdims=True)
            raised = jnp.exp2(scores - top)
            tops.append(top)
            sums.append(jnp.sum(raised, 0, keepdims=True))
            dots.append(jnp.sum(raised * dweights, 0, keepdims=True))
            pf[slot] = raised
            dpf[slot] = dweights
        top = functools.reduce(jnp.maximum, tops)
        factors = [jnp.exp2(t - top) for t in tops]
        inverse = 1.0 / sum(f * s for f, s in zip(factors, sums))
        row_dot = sum(f * d for f, d in zip(factors, dots)) * inverse
        columns = pl.ds(index * 2 * DIM, 2 * DIM)
        for slot in range(SLOTS):
            weights = pf[slot] * (factors[slot] * inverse)
            d_scores = weights * (dpf[slot] - row_dot)
            rows = pl.ds(slot * DIM, DIM)
            pt[rows, columns] = weights.astype(BF16)
            dst[rows, columns] = d_scores.astype(BF16)
        dq = contract(kt[...], dst[:, columns], ((1,), (0,))) * inv_root
        for i in range(2):
            at = pl.multiple_of((group * share + 2 * index + i) * DIM, DIM)
            dq_out[:, pl.ds(at, DIM)] = jnp.transpose(dq[:, i * DIM : (i + 1) * DIM]).astype(BF16)

    def one_group(group, carry):
        get_wait(group, 4)
        get_wait(group, 5)
        for slot in range(SLOTS):
            kt[:, slot * DIM : (slot + 1) * DIM] = jnp.transpose(kvb[group, slot, :, :DIM])
        for index in range(tiles):
            tile(group, index)
            if index == 0:

                @pl.when(group + 2 < kv_heads)
                def _():
                    relay(group + 2, 1)

                @pl.when(group + 1 < kv_heads)
                def _():
                    relay(group + 1, 3)

                @pl.when(group >= 1)
                def _():
                    ship(group - 1, 3, 6, False)

            if index == 1:

                @pl.when(group >= 2)
                def _():
                    settle(group - 2)

            if index == 2:

                @pl.when(group + 2 < kv_heads)
                def _():
                    relay(group + 2, 2)

                @pl.when(group >= 1)
                def _():
                    ship(group - 1, 2, 7, False)

        dv = contract(pt[...], stacked(gv, group, 0, share), ((1,), (0,)))
        dk = contract(dst[...], stacked(qv, group, 0, share), ((1,), (0,))) * inv_root
        for slot in range(SLOTS):
            rows = slice(slot * DIM, (slot + 1) * DIM)
            acc[group, slot, :, :DIM] = dk[rows]
            acc[group, slot, :, DIM:] = dv[rows]
        ship(group, 4, 5, True)

        @pl.when(group >= 1)
        def _():
            ship(group - 1, 1, 8, False)

        return carry

    lax.fori_loop(0, kv_heads, one_group, 0)

    last = kv_heads - 1
    ship(last, 3, 6, False)
    ship(last, 2, 7, False)
    settle(last - 1)
    ship(last, 1, 8, False)
    settle(last)
    for group in range(kv_heads):
        for lane in (0, 1, 2, 3, 8, 7, 6, 5):
            get_copy(group, 0, 1, 1, lane).wait_send()
        for slot in range(1, SLOTS):
            put_copy(group, slot, 0, 1).wait_send()


def body(queries, keys, values, grad_out, doc_ids):
    rows = queries.shape[0]
    heads = queries.shape[1] // DIM
    kv_heads = keys.shape[1] // DIM
    share = heads // kv_heads
    blks, swaps = lax.axis_size("blk"), lax.axis_size("swap")
    docs = doc_ids.reshape(blks * swaps, rows)
    hbm = pl.BlockSpec(memory_space=pl.ANY)
    vmem = pl.BlockSpec(memory_space=pltpu.VMEM)
    width = share * DIM
    return pl.pallas_call(
        functools.partial(kernel, blks, swaps, kv_heads, share),
        name="attention_backward",
        out_shape=(
            jax.ShapeDtypeStruct(queries.shape, BF16),
            jax.ShapeDtypeStruct(keys.shape, BF16),
            jax.ShapeDtypeStruct(values.shape, BF16),
        ),
        in_specs=[hbm, hbm, hbm, hbm, vmem],
        out_specs=(vmem, vmem, vmem),
        scratch_shapes=[
            pltpu.VMEM(queries.shape, BF16),
            pltpu.VMEM(queries.shape, BF16),
            pltpu.VMEM((kv_heads, SLOTS, DIM, 2 * DIM), BF16),
            pltpu.VMEM((DIM, SLOTS * DIM), BF16),
            pltpu.VMEM((SLOTS, DIM, DIM), F32),
            pltpu.VMEM((SLOTS, DIM, 2 * DIM), F32),
            pltpu.VMEM((SLOTS, DIM, 2 * DIM), F32),
            pltpu.VMEM((SLOTS * DIM, width), BF16),
            pltpu.VMEM((SLOTS * DIM, width), BF16),
            pltpu.VMEM((kv_heads, SLOTS, DIM, 2 * DIM), F32),
            pltpu.VMEM((kv_heads, SLOTS, DIM, 2 * DIM), BF16),
            pltpu.VMEM((kv_heads, SLOTS + 1, DIM, 2 * DIM), BF16),
            pltpu.SemaphoreType.DMA((2,)),
            pltpu.SemaphoreType.DMA((kv_heads, 2)),
            pltpu.SemaphoreType.DMA((kv_heads, SLOTS)),
            pltpu.SemaphoreType.DMA((kv_heads, SLOTS)),
            pltpu.SemaphoreType.DMA((kv_heads, SLOTS)),
            pltpu.SemaphoreType.DMA((kv_heads, SLOTS + 1)),
        ],
        compiler_params=pltpu.CompilerParams(
            collective_id=0, has_side_effects=True, vmem_limit_bytes=60 * 1024 * 1024
        ),
    )(queries, grad_out, keys, values, docs)


def solution(mesh):
    spec = P(("blk", "swap"), None)
    return jax.shard_map(
        body,
        mesh=mesh,
        in_specs=(spec, spec, spec, spec, P()),
        out_specs=(spec, spec, spec),
        check_vma=False,
    )
```

time: 321 us -> 107 us (0.33)
  the two profiles are of different devices: /device:TPU:4 before, /device:TPU:63 now
where the time goes in v1:
time: 107 us; the launch traced here: 106 us
  Pallas kernels  102 us (95%)
  local copies, waits for them, and re-layouts  3.93 us (4%)
    pallas_call x1, Pallas kernels, body(): pl.pallas_call(functools.partial(kernel, blks, swaps, kv_heads, share), n...  102 us
    unnamed x7, local copies, waits for them, and re-layouts  3.93 us

profile of v1, /device:TPU:63, one launch (start us, length us, event | category | flops | bytes accessed | tf_op | source)
XLA Modules:
  0.0 106.5 jit_solution(27029380677899250)
XLA Ops:
  0.6 101.9 %attention_backward.1 = (bf16[128,4096]{1,0:T(8,128)(2,1)}, bf16[128,512]{1,0:T(8,128)(2,1)}, bf16[128,512]{1,0:T(8,128)(2,1)}) custom-call(bf16[128,4096]{1,0:T(8,128)(2,1)} %q_hbm.1, bf16[128,4096]{1,0:T(8,128)(2,1)} %g_hbm.1, bf16[128,512]{1,0:T(8,128)(2,1)} %k_hbm.1, bf16[128,512]{1,0:T(8,128)(2,1)} %v_hbm.1, s32[256,128]{1,0:T(8,128)} %bitcast.1), custom_call_target="tpu_custom_call" | custom-call | tf_op jit(solution)/shard_map/attention_backward/pallas_call | solution.py:257
  102.5 0.0 copy-start.1
  102.6 2.3 %copy.11 = bf16[128,4096]{1,0:T(8,128)(2,1)} copy(bf16[128,4096]{1,0:T(8,128)(2,1)} %get-tuple-element.6) | data formatting | bytes 2097152
  104.9 0.0 copy-done.1
  104.9 0.0 copy-start
  104.9 0.7 copy.12
  105.5 0.3 copy-done
  105.8 0.7 copy.13
Async XLA Ops:
  102.5 2.3 %copy-start.1 = (bf16[128,512]{1,0:T(8,128)(2,1)S(1)}, bf16[128,512]{1,0:T(8,128)(2,1)}, u32[]{:S(2)}) copy-start(bf16[128,512]{1,0:T(8,128)(2,1)} %get-tuple-element.7) | copy-start | bytes 393220
  104.9 1.0 copy-start

commit v2 on v1

--- a/solution.py
+++ b/solution.py
@@ -19,6 +19,52 @@
 
 def contract(a, b, dims):
     return lax.dot_general(a, b, (dims, ((), ())), preferred_element_type=F32)
+
+
+def tree(cross):
+    parents = {}
+    for z in range(REACH):
+        for slot in range(1, SLOTS):
+            ours, block = (True, z - slot) if slot <= z else (False, z - slot + REACH)
+            rank = block if ours else REACH - 1 - block
+            far = (z if ours else REACH - 1 - z) > REACH // 2 + rank
+            if slot == REACH:
+                kind = "jump"
+            elif far and rank == 0:
+                kind = ("over_down" if z == REACH - 1 else "down") if ours else ("over_up" if z == 0 else "up")
+            elif far and rank <= cross:
+                kind = ("cross_down" if z == REACH - 1 else "down") if ours else ("cross_up" if z == 0 else "up")
+            else:
+                kind = "up" if ours else "down"
+            parents[slot, z] = kind
+    return parents
+
+
+STEP = {"up": 1, "down": -1, "over_up": 1 - REACH, "over_down": REACH - 1, "jump": REACH, "cross_up": 1, "cross_down": -1}
+SHIFT = {**STEP, "over_up": 1 - REACH, "over_down": REACH - 1}
+CROSS = 2
+LAG = 1
+SHIP_AT = (2,)
+PARENTS = tree(CROSS)
+
+
+def depth_of(slot, z):
+    if slot == 0:
+        return 0
+    kind = PARENTS[slot, z]
+    place = (z - STEP[kind]) % REACH
+    return 1 + depth_of(slot - SHIFT[kind], place)
+
+
+DEPTH = {key: depth_of(*key) for key in PARENTS}
+LAST = max(DEPTH.values())
+EDGES = sorted({(slot - SHIFT[kind], kind) for (slot, z), kind in PARENTS.items()})
+
+
+def senders(edge):
+    slot, kind = edge
+    child = slot + SHIFT[kind]
+    return frozenset((z - STEP[kind]) % REACH for z in range(REACH) if PARENTS.get((child, z)) == kind)
 
 
 def kernel(
@@ -30,9 +76,31 @@
 ):
     total = blks * swaps
     me = lax.axis_index("blk") * swaps + lax.axis_index("swap")
+    place = lax.rem(me, REACH)
     inv_root = 1.0 / math.sqrt(DIM)
     to_exp2 = inv_root * math.log2(math.e)
     tiles = share // 2
+
+    def among(places, run):
+        places = sorted(places)
+        if len(places) == REACH:
+            run()
+        elif places:
+            tests = []
+            start = previous = places[0]
+            for z in places[1:] + [None]:
+                if z is None or z != previous + 1:
+                    if start == previous:
+                        tests.append(place == start)
+                    elif start == 0:
+                        tests.append(place <= previous)
+                    elif previous == REACH - 1:
+                        tests.append(place >= start)
+                    else:
+                        tests.append((place >= start) & (place <= previous))
+                    start = z
+                previous = z
+            pl.when(functools.reduce(jnp.logical_or, tests))(run)
 
     def device(offset):
         other = lax.rem(me + (offset + total), total)
@@ -46,57 +114,76 @@
             own_sem.at[group, part],
         )
 
-    def get_copy(group, source, target, offset, lane):
+    def get_copy(group, edge):
+        slot, kind = EDGES[edge]
+        child = slot + SHIFT[kind]
         return pltpu.make_async_remote_copy(
-            src_ref=kvb.at[group, source],
-            dst_ref=kvb.at[group, target],
-            send_sem=get_send.at[group, lane],
-            recv_sem=get_recv.at[group, target],
-            device_id=device(offset),
+            src_ref=kvb.at[group, slot],
+            dst_ref=kvb.at[group, child],
+            send_sem=get_send.at[group, edge],
+            recv_sem=get_recv.at[group, child],
+            device_id=device(STEP[kind]),
             device_id_type=MESH,
         )
 
-    def put_copy(group, source, target, offset):
+    def put_copy(group, edge):
+        slot, kind = EDGES[edge]
+        child = slot + SHIFT[kind]
         return pltpu.make_async_remote_copy(
-            src_ref=outbox.at[group, source],
-            dst_ref=inbox.at[group, target],
-            send_sem=put_send.at[group, source],
-            recv_sem=put_recv.at[group, target],
-            device_id=device(offset),
+            src_ref=outbox.at[group, child],
+            dst_ref=inbox.at[group, edge],
+            send_sem=put_send.at[group, child],
+            recv_sem=put_recv.at[group, edge],
+            device_id=device(-STEP[kind]),
             device_id_type=MESH,
         )
 
-    def get_wait(group, slot):
-        get_copy(group, slot, slot, 1, 0).wait_recv()
-
-    def put_wait(group, slot):
-        put_copy(group, 1, slot, 1).wait_recv()
-
-    def relay(group, level):
-        near, far = level, SLOTS - level
-        get_wait(group, near)
-        get_copy(group, near, near + 1, 1, near).start()
-        get_wait(group, far)
-        get_copy(group, far, far - 1, -1, far - 1).start()
-
-    def ship(group, near, far, first):
-        for slot in (near, far):
-            value = acc[group, slot]
-            if not first:
-                put_wait(group, slot)
-                value = value + inbox[group, slot].astype(F32)
-            outbox[group, slot] = value.astype(BF16)
-            if slot == near:
-                put_copy(group, slot, slot - 1, -1).start()
-            elif slot < REACH:
-                put_copy(group, slot, slot + 1, 1).start()
-            else:
-                put_copy(group, slot, slot + 1, -REACH).start()
+    def receivers(edge):
+        slot, kind = EDGES[edge]
+        return frozenset((z + STEP[kind]) % REACH for z in senders(EDGES[edge]))
+
+    def forward(group, slot, places):
+        for edge, (source, _) in enumerate(EDGES):
+            if source == slot:
+                among(senders(EDGES[edge]) & places, lambda edge=edge: get_copy(group, edge).start())
+
+    def relay(group, depth):
+        for slot in range(1, SLOTS):
+            places = frozenset(z for z in range(REACH) if DEPTH[slot, z] == depth)
+
+            def run(slot=slot, places=places):
+                edge = next(e for e, (s, kind) in enumerate(EDGES) if s + SHIFT[kind] == slot)
+                get_copy(group, edge).wait_recv()
+                forward(group, slot, places)
+
+            among(places, run)
+
+    def gathered(group, slot, places):
+        for edge, (source, _) in enumerate(EDGES):
+            if source == slot:
+
+                def run(edge=edge):
+                    put_copy(group, edge).wait_recv()
+                    acc[group, slot] += inbox[group, edge].astype(F32)
+
+                among(senders(EDGES[edge]) & places, run)
+
+    def ship(group, depth):
+        for slot in range(1, SLOTS):
+            places = frozenset(z for z in range(REACH) if DEPTH[slot, z] == depth)
+
+            def run(slot=slot, places=places):
+                gathered(group, slot, places)
+                outbox[group, slot] = acc[group, slot].astype(BF16)
+                for edge, (source, kind) in enumerate(EDGES):
+                    if source + SHIFT[kind] == slot:
+                        among(receivers(edge) & places, lambda edge=edge: put_copy(group, edge).start())
+
+            among(places, run)
 
     def settle(group):
-        put_wait(group, 0)
-        put_wait(group, SLOTS)
-        value = acc[group, 0] + inbox[group, 0].astype(F32) + inbox[group, SLOTS].astype(F32)
+        gathered(group, 0, frozenset(range(REACH)))
+        value = acc[group, 0]
         at = pl.multiple_of(group * DIM, DIM)
         dk_out[:, pl.ds(at, DIM)] = value[:, :DIM].astype(BF16)
         dv_out[:, pl.ds(at, DIM)] = value[:, DIM:].astype(BF16)
@@ -110,15 +197,15 @@
     g_load.start()
 
     barrier = pltpu.get_barrier_semaphore()
-    for offset in (1, -1, REACH, -REACH):
+    offsets = (1, -1, REACH, -REACH, REACH - 1, 1 - REACH)
+    for offset in offsets:
         pl.semaphore_signal(barrier, inc=1, device_id=device(offset), device_id_type=MESH)
-    pl.semaphore_wait(barrier, 4)
+    pl.semaphore_wait(barrier, len(offsets))
 
     for group in range(kv_heads):
         for part in range(2):
             own_copy(group, part).wait()
-        get_copy(group, 0, 1, 1, 0).start()
-        get_copy(group, 0, REACH, REACH, REACH).start()
+        forward(group, 0, frozenset(range(REACH)))
 
     q_docs = docs[pl.ds(me, 1), :].astype(F32)
     causal = lax.broadcasted_iota(jnp.int32, (DIM, DIM), 0) <= lax.broadcasted_iota(
@@ -135,10 +222,10 @@
     q_load.wait()
     g_load.wait()
 
-    for level in range(1, 4):
-        relay(0, level)
-        if level > 1 and kv_heads > 1:
-            relay(1, level - 1)
+    for depth in range(1, LAST + 1):
+        for group in range(kv_heads):
+            if depth - LAG * group >= 1:
+                relay(group, depth - LAG * group)
 
     def stacked(ref, group, first, count):
         at = (group * share + first) * DIM
@@ -179,41 +266,26 @@
             dq_out[:, pl.ds(at, DIM)] = jnp.transpose(dq[:, i * DIM : (i + 1) * DIM]).astype(BF16)
 
     def one_group(group, carry):
-        get_wait(group, 4)
-        get_wait(group, 5)
         for slot in range(SLOTS):
             kt[:, slot * DIM : (slot + 1) * DIM] = jnp.transpose(kvb[group, slot, :, :DIM])
         for index in range(tiles):
             tile(group, index)
-            if index == 0:
-
-                @pl.when(group + 2 < kv_heads)
-                def _():
-                    relay(group + 2, 1)
-
-                @pl.when(group + 1 < kv_heads)
-                def _():
-                    relay(group + 1, 3)
-
-                @pl.when(group >= 1)
-                def _():
-                    ship(group - 1, 3, 6, False)
-
-            if index == 1:
-
-                @pl.when(group >= 2)
-                def _():
-                    settle(group - 2)
-
-            if index == 2:
-
-                @pl.when(group + 2 < kv_heads)
-                def _():
-                    relay(group + 2, 2)
-
-                @pl.when(group >= 1)
-                def _():
-                    ship(group - 1, 2, 7, False)
+            if index % 2 == 0 and index // 2 < LAG:
+                for ahead in range(1, kv_heads):
+                    depth = LAST - LAG * ahead + index // 2 + 1
+                    if depth >= 1:
+                        pl.when(group + ahead < kv_heads)(
+                            lambda ahead=ahead, depth=depth: relay(group + ahead, depth)
+                        )
+            if index in SHIP_AT:
+                for behind in range(1, kv_heads):
+                    depth = LAST - (len(SHIP_AT) * (behind - 1) + SHIP_AT.index(index)) - 1
+                    if depth >= 1:
+                        pl.when(group >= behind)(
+                            lambda behind=behind, depth=depth: ship(group - behind, depth)
+                        )
+                    elif depth == 0:
+                        pl.when(group >= behind)(lambda behind=behind: settle(group - behind))
 
         dv = contract(pt[...], stacked(gv, group, 0, share), ((1,), (0,)))
         dk = contract(dst[...], stacked(qv, group, 0, share), ((1,), (0,))) * inv_root
@@ -221,27 +293,22 @@
             rows = slice(slot * DIM, (slot + 1) * DIM)
             acc[group, slot, :, :DIM] = dk[rows]
             acc[group, slot, :, DIM:] = dv[rows]
-        ship(group, 4, 5, True)
-
-        @pl.when(group >= 1)
-        def _():
-            ship(group - 1, 1, 8, False)
-
+        ship(group, LAST)
         return carry
 
     lax.fori_loop(0, kv_heads, one_group, 0)
 
-    last = kv_heads - 1
-    ship(last, 3, 6, False)
-    ship(last, 2, 7, False)
-    settle(last - 1)
-    ship(last, 1, 8, False)
-    settle(last)
+    for index in range(LAST):
+        for group in range(kv_heads):
+            depth = LAST - 1 - (len(SHIP_AT) * (kv_heads - 1 - group) + index)
+            if depth >= 1:
+                ship(group, depth)
+            elif depth == 0:
+                settle(group)
     for group in range(kv_heads):
-        for lane in (0, 1, 2, 3, 8, 7, 6, 5):
-            get_copy(group, 0, 1, 1, lane).wait_send()
-        for slot in range(1, SLOTS):
-            put_copy(group, slot, 0, 1).wait_send()
+        for edge in range(len(EDGES)):
+            among(senders(EDGES[edge]), lambda group=group, edge=edge: get_copy(group, edge).wait_send())
+            among(receivers(edge), lambda group=group, edge=edge: put_copy(group, edge).wait_send())
 
 
 def body(queries, keys, values, grad_out, doc_ids):
@@ -276,13 +343,13 @@
             pltpu.VMEM((SLOTS * DIM, width), BF16),
             pltpu.VMEM((kv_heads, SLOTS, DIM, 2 * DIM), F32),
             pltpu.VMEM((kv_heads, SLOTS, DIM, 2 * DIM), BF16),
-            pltpu.VMEM((kv_heads, SLOTS + 1, DIM, 2 * DIM), BF16),
+            pltpu.VMEM((kv_heads, len(EDGES), DIM, 2 * DIM), BF16),
             pltpu.SemaphoreType.DMA((2,)),
             pltpu.SemaphoreType.DMA((kv_heads, 2)),
+            pltpu.SemaphoreType.DMA((kv_heads, len(EDGES))),
             pltpu.SemaphoreType.DMA((kv_heads, SLOTS)),
             pltpu.SemaphoreType.DMA((kv_heads, SLOTS)),
-            pltpu.SemaphoreType.DMA((kv_heads, SLOTS)),
-            pltpu.SemaphoreType.DMA((kv_heads, SLOTS + 1)),
+            pltpu.SemaphoreType.DMA((kv_heads, len(EDGES))),
         ],
         compiler_params=pltpu.CompilerParams(
             collective_id=0, has_side_effects=True, vmem_limit_bytes=60 * 1024 * 1024

time: 107 us -> 94.1 us (0.88)
  the two profiles are of different devices: /device:TPU:63 before, /device:TPU:4 now
where the time goes in v2:
time: 94.1 us; the launch traced here: 93.6 us
  Pallas kernels  89 us (95%)
  local copies, waits for them, and re-layouts  3.93 us (4%)
    pallas_call x1, Pallas kernels, body(): pl.pallas_call(functools.partial(kernel, blks, swaps, kv_heads, share), n...  89 us
    unnamed x7, local copies, waits for them, and re-layouts  3.93 us

profile of v2, /device:TPU:4, one launch (start us, length us, event | category | flops | bytes accessed | tf_op | source)
XLA Modules:
  0.0 93.6 jit_solution(15415313676648624130)
XLA Ops:
  0.6 89.0 %attention_backward.1 = (bf16[128,4096]{1,0:T(8,128)(2,1)}, bf16[128,512]{1,0:T(8,128)(2,1)}, bf16[128,512]{1,0:T(8,128)(2,1)}) custom-call(bf16[128,4096]{1,0:T(8,128)(2,1)} %q_hbm.1, bf16[128,4096]{1,0:T(8,128)(2,1)} %g_hbm.1, bf16[128,512]{1,0:T(8,128)(2,1)} %k_hbm.1, bf16[128,512]{1,0:T(8,128)(2,1)} %v_hbm.1, s32[256,128]{1,0:T(8,128)} %bitcast.1), custom_call_target="tpu_custom_call" | custom-call | tf_op jit(solution)/shard_map/attention_backward/pallas_call | solution.py:324
  89.7 0.0 copy-start.1
  89.7 2.3 %copy.11 = bf16[128,4096]{1,0:T(8,128)(2,1)} copy(bf16[128,4096]{1,0:T(8,128)(2,1)} %get-tuple-element.6) | data formatting | bytes 2097152
  92.0 0.0 copy-done.1
  92.0 0.0 copy-start
  92.0 0.7 copy.12
  92.7 0.3 copy-done
  93.0 0.7 copy.13
Async XLA Ops:
  89.7 2.3 %copy-start.1 = (bf16[128,512]{1,0:T(8,128)(2,1)S(1)}, bf16[128,512]{1,0:T(8,128)(2,1)}, u32[]{:S(2)}) copy-start(bf16[128,512]{1,0:T(8,128)(2,1)} %get-tuple-element.7) | copy-start | bytes 393220
  92.0 1.0 %copy-start = (bf16[128,512]{1,0:T(8,128)(2,1)S(1)}, bf16[128,512]{1,0:T(8,128)(2,1)}, u32[]{:S(2)}) copy-start(bf16[128,512]{1,0:T(8,128)(2,1)} %get-tuple-element.8) | copy-start | bytes 393220

commit v3 on v2

--- a/solution.py
+++ b/solution.py
@@ -44,7 +44,7 @@
 SHIFT = {**STEP, "over_up": 1 - REACH, "over_down": REACH - 1}
 CROSS = 2
 LAG = 1
-SHIP_AT = (2,)
+SHIP_AT = (3,)
 PARENTS = tree(CROSS)
 
 
@@ -270,9 +270,9 @@
             kt[:, slot * DIM : (slot + 1) * DIM] = jnp.transpose(kvb[group, slot, :, :DIM])
         for index in range(tiles):
             tile(group, index)
-            if index % 2 == 0 and index // 2 < LAG:
+            if index == 1:
                 for ahead in range(1, kv_heads):
-                    depth = LAST - LAG * ahead + index // 2 + 1
+                    depth = LAST - LAG * ahead + 1
                     if depth >= 1:
                         pl.when(group + ahead < kv_heads)(
                             lambda ahead=ahead, depth=depth: relay(group + ahead, depth)

time: 94.1 us -> 94.6 us (level); the launches traced: 93.6 us -> 93 us
  no operation moved by 1% of the time
where the time goes in v3:
time: 94.6 us; the launch traced here: 93 us
  Pallas kernels  88.4 us (93%)
  local copies, waits for them, and re-layouts  3.93 us (4%)
    pallas_call x1, Pallas kernels, body(): pl.pallas_call(functools.partial(kernel, blks, swaps, kv_heads, share), n...  88.4 us
    unnamed x7, local copies, waits for them, and re-layouts  3.93 us

profile of v3, /device:TPU:4, one launch (start us, length us, event | category | flops | bytes accessed | tf_op | source)
XLA Modules:
  0.0 93.0 jit_solution(14532203510598994137)
XLA Ops:
  0.6 88.4 %attention_backward.1 = (bf16[128,4096]{1,0:T(8,128)(2,1)}, bf16[128,512]{1,0:T(8,128)(2,1)}, bf16[128,512]{1,0:T(8,128)(2,1)}) custom-call(bf16[128,4096]{1,0:T(8,128)(2,1)} %q_hbm.1, bf16[128,4096]{1,0:T(8,128)(2,1)} %g_hbm.1, bf16[128,512]{1,0:T(8,128)(2,1)} %k_hbm.1, bf16[128,512]{1,0:T(8,128)(2,1)} %v_hbm.1, s32[256,128]{1,0:T(8,128)} %bitcast.1), custom_call_target="tpu_custom_call" | custom-call | tf_op jit(solution)/shard_map/attention_backward/pallas_call | solution.py:324
  89.1 0.0 copy-start.1
  89.1 2.3 %copy.11 = bf16[128,4096]{1,0:T(8,128)(2,1)} copy(bf16[128,4096]{1,0:T(8,128)(2,1)} %get-tuple-element.6) | data formatting | bytes 2097152
  91.4 0.0 copy-done.1
  91.4 0.0 copy-start
  91.4 0.7 copy.12
  92.1 0.3 copy-done
  92.4 0.7 copy.13
Async XLA Ops:
  89.1 2.3 %copy-start.1 = (bf16[128,512]{1,0:T(8,128)(2,1)S(1)}, bf16[128,512]{1,0:T(8,128)(2,1)}, u32[]{:S(2)}) copy-start(bf16[128,512]{1,0:T(8,128)(2,1)} %get-tuple-element.7) | copy-start | bytes 393220
  91.4 1.0 %copy-start = (bf16[128,512]{1,0:T(8,128)(2,1)S(1)}, bf16[128,512]{1,0:T(8,128)(2,1)}, u32[]{:S(2)}) copy-start(bf16[128,512]{1,0:T(8,128)(2,1)} %get-tuple-element.8) | copy-start | bytes 393220
